TPU v7x, 32 devices: a whole 2x2x4 slice. The times are simulated.
32 devices in a mesh: group: 2 (over y), sta: 4 (over z), win: 2 (over x), freq: 2 (over core).
Axes of the slice: x: 2, y: 2, z: 4, core: 2. Of those that a mesh axis runs over, the one named last changes fastest.
Arguments:
- records: float32 [1024, 4, 3600], P(('group', 'sta'), 'win', 'freq'), parts along dimension 0, may hold values from -6 to 6
- valid_counts: int32 [8], P(('group', 'sta')), parts along dimension 0, may hold values from 64 to 128, as said below
- pair_blocks: int32 [8, 2], P('group'), parts along dimension 0, may hold values from 0 to 3, as said below
Outputs:
- pair_spectra: bfloat16 [8, 2, 256, 2, 128, 128], P(('group', 'sta'), 'freq', 'win'), parts along dimension 0
There are 2 independent parts, one for each index of `group`. A program takes and returns all parts, laid end to end along the dimension named above; each array names one. Nothing has to cross between parts.
Inputs may be any that keep to these rules, and one draw needn't show every extreme that they name: The stations of block i at positions below valid_counts[i] are live, the others are masked out. `pair_blocks`: slot k belongs to index k // 1 of sta and names two station blocks.
All inputs are finite; a program needn't handle non-finite values.
Results may differ from a plain program's by a relative error of at most 0.001.
Values may be sent and summed in bfloat16 or wider, within the bound.
A program may use at most 64 MiB of HBM per device.

v0:
```python
import math

import jax
import jax.numpy as jnp
from jax import lax
from jax.sharding import PartitionSpec as P

SAMPLES = 3600
BINS = 512
HALF_WIDTH = 10


TWO_PI = 2.0 * math.pi
AMP_FLOOR = 0.1
PRECISE = lax.Precision.HIGHEST


def padded_2(value, sides, width):
    for axis, dim in sides:
        peers, length = (lax.axis_size(axis), value.shape[dim])
        up = [(i, (i + 1) % peers) for i in range(peers - 1)]
        down = [(j, i) for i, j in up]
        last = lax.slice_in_dim(value, length - width, length, axis=dim)
        first = lax.slice_in_dim(value, 0, width, axis=dim)
        before = lax.ppermute(last, axis, up)
        after = lax.ppermute(first, axis, down)
        value = jnp.concatenate([before, value, after], axis=dim)
    return value


def taper_of(sample_index, length_all):
    edge_len = length_all // 20
    position = jnp.minimum(sample_index, length_all - 1 - sample_index)
    ramped = 0.5 * (1.0 - jnp.cos(math.pi * (position.astype(jnp.float32) + 0.5) / edge_len))
    return jnp.where(position < edge_len, ramped, 1.0)


def dft_tables(bin_start, amount, sample_count, length_all):
    bin_index = bin_start + 1 + lax.broadcasted_iota(jnp.int32, (amount, sample_count), 0)
    sample_index = lax.broadcasted_iota(jnp.int32, (amount, sample_count), 1)
    angles = (bin_index * sample_index % length_all).astype(jnp.float32) * (TWO_PI / length_all)
    weight = taper_of(sample_index, length_all) / math.sqrt(length_all)
    return (jnp.cos(angles) * weight, -jnp.sin(angles) * weight)


def cross_pair(left_block, right_block):
    left_real = left_block[:, :, 0]
    left_imag = left_block[:, :, 1]
    stacked = jnp.stack(
        (jnp.stack((left_real, left_imag), 2), jnp.stack((left_imag, -left_real), 2)), 1
    )
    factor = 1.0 / math.sqrt(left_block.shape[1])
    return jnp.einsum("fpwqa,fwqb->fpab", stacked, right_block, precision=PRECISE) * factor


def local(records, valid_counts, pair_blocks):
    block_size = records.shape[0]
    band_bins = BINS // lax.axis_size("freq")
    first_bin = lax.axis_index("freq") * band_bins
    portion = lax.all_gather(records, "freq", axis=2, tiled=True)
    cos_table, sin_table = dft_tables(first_bin, band_bins, portion.shape[2], SAMPLES)
    real_part = jnp.einsum("kn,swn->kws", cos_table, portion, precision=PRECISE)
    imag_part = jnp.einsum("kn,swn->kws", sin_table, portion, precision=PRECISE)
    spectrum = jnp.stack((real_part, imag_part), 2)
    live_mask = (lax.broadcasted_iota(jnp.int32, (block_size,), 0) < valid_counts[0]).astype(
        jnp.float32
    )
    spectrum = spectrum * live_mask
    magnitude = jnp.sqrt(
        spectrum[:, :, 0] * spectrum[:, :, 0] + spectrum[:, :, 1] * spectrum[:, :, 1]
    )
    padded = padded_2(magnitude, (("freq", 0),), HALF_WIDTH)
    row_index = lax.broadcasted_iota(jnp.int32, (band_bins, band_bins + 2 * HALF_WIDTH), 0)
    col_index = lax.broadcasted_iota(jnp.int32, (band_bins, band_bins + 2 * HALF_WIDTH), 1)
    box_matrix = ((col_index - row_index >= 0) & (col_index - row_index <= 2 * HALF_WIDTH)).astype(
        jnp.float32
    )
    summed = jnp.einsum("ij,jws->iws", box_matrix, padded, precision=PRECISE)
    global_bin = first_bin + lax.broadcasted_iota(jnp.int32, (band_bins,), 0)
    counted = (
        jnp.minimum(global_bin + HALF_WIDTH, BINS - 1) - jnp.maximum(global_bin - HALF_WIDTH, 0) + 1
    ).astype(jnp.float32)
    smooth = summed / counted[:, None, None]
    whitened = spectrum / jnp.maximum(smooth, AMP_FLOOR)[:, :, None, :]
    sta_count = lax.axis_size("sta")
    slots = pair_blocks.shape[0] // sta_count
    my_slots = lax.dynamic_slice_in_dim(pair_blocks, lax.axis_index("sta") * slots, slots, 0)
    held_block = lax.all_to_all(whitened, "win", split_axis=0, concat_axis=1, tiled=True)
    blank_pair = jnp.zeros((slots,) + held_block.shape, jnp.float32)
    carried = (blank_pair, blank_pair)
    portion = lax.all_gather(held_block[None], "sta", axis=0, tiled=True)
    amount = portion.shape[0]
    chosen = []
    for column in range(2):
        wanted = my_slots[:, column]
        inside = (wanted >= 0) & (wanted < amount)
        fetched = jnp.take(portion, jnp.clip(wanted, 0, amount - 1), axis=0)
        chosen.append(jnp.where(inside[:, None, None, None, None], fetched, carried[column]))
    left_blocks = chosen[0]
    right_blocks = chosen[1]
    mixed = jax.vmap(cross_pair)(left_blocks, right_blocks).astype(jnp.bfloat16)
    return mixed[:, None]


def solution(mesh):
    in_specs = (P(("group", "sta"), "win", "freq"), P(("group", "sta")), P("group", None))
    out_specs = P(("group", "sta"), "freq", "win", None, None, None)
    return jax.shard_map(local, mesh=mesh, in_specs=in_specs, out_specs=out_specs, check_vma=False)
```

profile of v0, /device:TPU:0, one launch (start us, length us, event | category | flops | bytes accessed | tf_op | source)
XLA Modules:
  0.0 175.7 jit_solution(15182454830260234039)
XLA Ops:
  6.5 0.0 copy-start
  6.5 0.0 all-gather.3.cloned.1.call-start
  6.5 0.7 all-gather.3.cloned.1.call-update
  7.3 0.0 all-gather.5.cloned.1.call-start
  8.0 0.1 subtract_multiply_fusion
  8.1 16.5 %all-gather.3.cloned.1.call-done = f32[128,2,3600]{0,2,1:T(8,128)} async-done(((f32[128,2,1800]{0,2,1:T(8,128)}), f32[128,2,3600]{0,2,1:T(8,128)}) %all-gather.3.cloned.1.call-update) | async-done | bytes 3686416 | tf_op jit(solution)/shard_map/all_gather | solution.py:60
  24.6 0.0 copy-start.1
  24.6 25.0 %fusion.37 = f32[256,2,1,128]{3,0,1,2:T(8,128)S(1)} fusion(f32[128,2,3600]{0,2,1:T(8,128)} %all-gather.3.cloned.1.call-done, f32[3600]{0:T(1024)S(1)} %subtract_multiply_fusion, s32[256]{0:T(256)S(1)} %iota_add_fusion, pred[3600]{0:T(1024)(128)(4,1)S(1)} %fusion.65), kind=kOutput, calls=%fused_computation.35 | convolution fusion | flops 2843136000 | bytes 3967568 | tf_op jit(solution)/shard_map/kn,swn->kws/dot_general | solution.py:63
  49.6 0.0 copy-done.1
  49.6 21.3 %fusion.34 = f32[256,2,1,128]{3,0,1,2:T(8,128)S(1)} fusion(f32[128,2,3600]{0,2,1:T(8,128)S(1)} %copy-done.1, f32[3600]{0:T(1024)S(1)} %subtract_multiply_fusion, s32[256]{0:T(256)S(1)} %iota_add_fusion, pred[3600]{0:T(1024)(128)(4,1)S(1)} %fusion.65), kind=kOutput, calls=%fused_computation.34 | convolution fusion | flops 2842214400 | bytes 3967568 | tf_op jit(solution)/shard_map/kn,swn->kws/dot_general | solution.py:62
  70.9 0.1 fusion.58
  71.1 2.1 %collective-permute-start = (f32[10,2,128]{2,0,1:T(8,128)S(1)}, f32[10,2,128]{2,0,1:T(8,128)S(1)}, u32[]{:S(2)}, u32[]{:S(2)}) collective-permute-start(f32[10,2,128]{2,0,1:T(8,128)S(1)} %get-tuple-element.21), channel_id=1, source_target_pairs={{0,1},{2,3},{4,5},{6,7},{8,9},{10,11},{12,13},{14,15},{16,17},{18,... | collective-permute-start | bytes 30728 | tf_op jit(solution)/shard_map/ppermute | solution.py:25
  73.2 1.3 collective-permute-start.1
  74.5 0.1 fusion.86
  74.6 0.0 collective-permute-done
  74.6 1.7 collective-permute-done.1
  76.3 0.5 fusion.40
  76.8 0.1 broadcast_divide_fusion
  76.8 0.4 copy.6
  77.3 11.3 %all_to_all.15 = f32[256,2,2,128]{3,1,2,0:T(2,128)S(1)} all-to-all(f32[256,2,2,128]{3,1,2,0:T(2,128)S(1)} %copy.6), channel_id=1, replica_groups=mesh['group'=2,'sta'=4,'win'=2,'freq'=2] {'win'}, dimensions={0} | all-to-all | bytes 1048576 | tf_op jit(solution)/shard_map/all_to_all | solution.py:88
  88.5 0.8 copy.7
  89.3 0.0 all-gather.5.cloned.1.call-update
  89.4 0.0 copy-done
  89.4 0.1 constant_dynamic-slice_fusion.2
  89.4 0.5 fusion.82
  93.5 42.0 %all-gather.5.cloned.1.call-done = f32[4,128,4,2,128]{4,1,3,2,0:T(8,128)} async-done(((f32[1,128,4,2,128]{4,1,3,2,0:T(8,128)}), f32[4,128,4,2,128]{4,1,3,2,0:T(8,128)}) %all-gather.5.cloned.1.call-update) | async-done | bytes 2097168 | tf_op jit(solution)/shard_map/all_gather | solution.py:91
  135.6 1.3 constant_dynamic-slice_fusion
  136.8 0.5 fusion.85
  137.3 0.5 fusion.45
  137.8 0.1 fusion.81
  137.9 0.1 maximum_bitcast_fusion.1
  138.0 30.8 %fusion.1 = bf16[1,1,128,2,128,128]{5,4,3,2,1,0:T(8,128)(2,1)} fusion(f32[1,128,4,2,128]{4,1,3,2,0:T(8,128)S(1)} %get-tuple-element.17, pred[]{:T(512)} %bitcast.23, pred[]{:T(512)} %bitcast.21, f32[1,128,1,4,2,128]{5,3,4,1,2,0:T(4,128)S(1)} %maximum_bitcast_fusion.1, f32[1,128,1,4,2,128]{5,3,4,1,2,0:T(4,128)S(1)} %fusion.85), kind=kOutput, calls=%fused_computation.3 | convolution fusion | flops 411566080 | bytes 9961474 | tf_op jit(solution)/shard_map/vmap(fpwqa,fwqb->fpab)/dot_general | solution.py:53
  (6 shorter events, 0.1 us)
Async XLA Ops:
  6.5 82.8 %copy-start = (s32[4,2]{0,1:T(2,128)S(1)}, s32[4,2]{0,1:T(2,128)}, u32[]{:S(2)}) copy-start(s32[4,2]{0,1:T(2,128)} %param.7) | copy-start | bytes 100
  6.5 18.0 %all-gather.3.cloned.1.call-start = ((), (), s32[]{:S(2)}) async-start(), calls=%async_computation.1 | async-start | bytes 5529600 | tf_op jit(solution)/shard_map/all_gather | solution.py:60
  7.3 128.3 %all-gather.5.cloned.1.call-start = ((), (), s32[]{:S(2)}) async-start(), calls=%async_computation.2 | async-start | bytes 2621440 | tf_op jit(solution)/shard_map/all_gather | solution.py:91
  24.6 25.0 %copy-start.1 = (f32[128,2,3600]{0,2,1:T(8,128)S(1)}, f32[128,2,3600]{0,2,1:T(8,128)}, u32[]{:S(2)}) copy-start(f32[128,2,3600]{0,2,1:T(8,128)} %all-gather.3.cloned.1.call-done) | copy-start | bytes 11059204
  71.1 3.5 %collective-permute-start = (f32[10,2,128]{2,0,1:T(8,128)S(1)}, f32[10,2,128]{2,0,1:T(8,128)S(1)}, u32[]{:S(2)}, u32[]{:S(2)}) collective-permute-start(f32[10,2,128]{2,0,1:T(8,128)S(1)} %get-tuple-element.21), channel_id=1, source_target_pairs={{0,1},{2,3},{4,5},{6,7},{8,9},{10,11},{12,13},{14,15},{16,17},{18,... | collective-permute-start | bytes 30728 | tf_op jit(solution)/shard_map/ppermute | solution.py:25
  73.2 3.1 %collective-permute-start.1 = (f32[10,2,128]{2,0,1:T(8,128)S(1)}, f32[10,2,128]{2,0,1:T(8,128)S(1)}, u32[]{:S(2)}, u32[]{:S(2)}) collective-permute-start(f32[10,2,128]{2,0,1:T(8,128)S(1)} %get-tuple-element.22), channel_id=1, source_target_pairs={{1,0},{3,2},{5,4},{7,6},{9,8},{11,10},{13,12},{15,14},{17,16},{19,... | collective-permute-start | bytes 30728 | tf_op jit(solution)/shard_map/ppermute | solution.py:26
Sparse Core Ops, SparseCore 0:
  8.9 15.6 all-gather.2
  89.5 46.0 all-gather.4
where the time goes:
time: 176 us
  matrix products  77.6 us (44%)
  waiting for transfers between devices  60.9 us (35%)
  between operations  17.8 us (10%)
  blocking collectives  11.3 us (6%)
  starting transfers between devices  3.45 us (2%)
  local copies, waits for them, and re-layouts  3.12 us (2%)
    all_gather x1, waiting for transfers between devices, local(): portion = lax.all_gather(held_block[None], 'sta', axis=0, tiled=True)  42 us
    dot_general x1, matrix products, cross_pair(): jnp.einsum('fpwqa,fwqb->fpab', stacked, right_block, precision=PRECISE)  30.8 us
    dot_general x1, matrix products, local(): imag_part = jnp.einsum('kn,swn->kws', sin_table, portion, precision=PRECISE)  25 us
    dot_general x1, matrix products, local(): real_part = jnp.einsum('kn,swn->kws', cos_table, portion, precision=PRECISE)  21.3 us
    all_gather x1, waiting for transfers between devices, local(): portion = lax.all_gather(records, 'freq', axis=2, tiled=True)  16.5 us
    all_to_all x1, blocking collectives, local(): lax.all_to_all(whitened, 'win', split_axis=0, concat_axis=1, tiled=True)  11.3 us
  transfers between devices with their start and end apart: 4, of which 3 were waited for; matrix products, arithmetic and copies ran while one was open for 0% of the time, Pallas kernels for 0%

commit v1 on v0

v1 whole, which is shorter than its diff:
```python
import functools
import math

import jax
import jax.numpy as jnp
import numpy as np
from jax import lax
from jax.experimental import pallas as pl
from jax.experimental.pallas import tpu as pltpu
from jax.sharding import PartitionSpec as P

SAMPLES = 3600
BINS = 512
HALF_WIDTH = 10
AMP_FLOOR = 0.1
HALO = 16
PAD = 1920
BAND = BINS // 2
ROWS = BAND + HALO
LEVELS = 32766.0
MESH = pl.DeviceIdType.MESH


def band_bins(band):
    own = np.arange(BAND) + band * BAND
    halo = np.arange(HALO) + (BAND if band == 0 else BAND - HALO)
    return np.concatenate([own, halo])


def dft_table():
    half = SAMPLES // 2
    table = np.zeros((2, 2, 2, ROWS, PAD), jnp.bfloat16)
    for band in range(2):
        phase = (band_bins(band)[:, None] + 1) * np.arange(half)[None] % SAMPLES
        angle = phase * (2.0 * math.pi / SAMPLES)
        for part, value in enumerate((np.cos(angle), -np.sin(angle))):
            high = value.astype(jnp.bfloat16)
            table[band, part, 0, :, :half] = high
            table[band, part, 1, :, :half] = (value - high.astype(np.float64)).astype(jnp.bfloat16)
    return table


def split(value):
    high = value.astype(jnp.bfloat16)
    return high, (value - high.astype(jnp.float32)).astype(jnp.bfloat16)


def dot_nt(a, b):
    return lax.dot_general(a, b, (((1,), (1,)), ((), ())), preferred_element_type=jnp.float32)


def spectra_kernel(
    stas, wins, local_wins, x_ref, table_ref, out_ref,
    tab, xh, xl, give, got, own, codes,
    tab_sem, fs_sem, fr_sem, ws_sem, wr_sem, rs_sem, rr_sem, ls_sem, lr_sem, own_sem,
):
    sta = lax.axis_index("sta")
    win = lax.axis_index("win")
    freq = lax.axis_index("freq")
    other = 1 - freq
    cols = x_ref.shape[0]
    lanes = cols // local_wins
    sub = BAND // wins
    has_right = sta < stas - 1
    has_left = sta > 0

    def table_copy(step):
        band = other if step < 2 else freq
        return pltpu.make_async_copy(
            table_ref.at[band, step % 2], tab.at[step], tab_sem.at[step]
        )

    for step in range(4):
        table_copy(step).start()

    barrier = pltpu.get_barrier_semaphore()
    pl.semaphore_signal(barrier, inc=1, device_id={"freq": other}, device_id_type=MESH)
    for hop in range(1, wins):
        pl.semaphore_signal(
            barrier, inc=1, device_id={"win": lax.rem(win + hop, wins)}, device_id_type=MESH
        )

    @pl.when(has_right)
    def _():
        pl.semaphore_signal(barrier, inc=1, device_id={"sta": sta + 1}, device_id_type=MESH)

    @pl.when(has_left)
    def _():
        pl.semaphore_signal(barrier, inc=1, device_id={"sta": sta - 1}, device_id_type=MESH)

    high, low = split(x_ref[...])
    xh[...] = high
    xl[...] = low

    ends = jnp.where(has_right, 1, 0) + jnp.where(has_left, 1, 0)
    pl.semaphore_wait(barrier, wins + ends)

    odd = lax.broadcasted_iota(jnp.int32, (ROWS, 1), 0) % 2
    sign = jnp.where((odd == 0) & (freq == 1), -1.0, 1.0).astype(jnp.float32)

    def partial(step):
        table_copy(step).wait()
        value = dot_nt(tab[step, 0], xh[...]) + (
            dot_nt(tab[step, 0], xl[...]) + dot_nt(tab[step, 1], xh[...])
        )
        return value * sign

    def freq_copy(step):
        return pltpu.make_async_remote_copy(
            src_ref=give.at[step], dst_ref=got.at[step],
            send_sem=fs_sem.at[step], recv_sem=fr_sem.at[step],
            device_id={"freq": other}, device_id_type=MESH,
        )

    for step in range(2):
        give[step] = partial(step)
        freq_copy(step).start()
    for step in range(2):
        own[step] = partial(2 + step)
    for step in range(2):
        freq_copy(step).wait()

    real = own[0] + got[0]
    imag = own[1] + got[1]
    magnitude = jnp.sqrt(real * real + imag * imag)
    row = lax.broadcasted_iota(jnp.int32, (BAND, ROWS), 0)
    col = lax.broadcasted_iota(jnp.int32, (BAND, ROWS), 1)
    place = jnp.where(col < BAND, col, jnp.where(freq == 0, col, col - BAND - HALO))
    box = ((place - row <= HALF_WIDTH) & (row - place <= HALF_WIDTH)).astype(jnp.float32)
    box = box.astype(jnp.bfloat16)
    mag_high, mag_low = split(magnitude)
    summed = jnp.dot(box, mag_high, preferred_element_type=jnp.float32) + jnp.dot(
        box, mag_low, preferred_element_type=jnp.float32
    )
    bin_at = freq * BAND + lax.broadcasted_iota(jnp.int32, (BAND, 1), 0)
    counted = (
        jnp.minimum(bin_at + HALF_WIDTH, BINS - 1) - jnp.maximum(bin_at - HALF_WIDTH, 0) + 1
    ).astype(jnp.float32)
    inverse = 1.0 / jnp.maximum(summed / counted, AMP_FLOOR)
    real = real[:BAND] * inverse
    imag = imag[:BAND] * inverse

    for dest in range(wins):
        for w in range(local_wins):
            re = real[dest * sub:(dest + 1) * sub, w * lanes:(w + 1) * lanes]
            im = imag[dest * sub:(dest + 1) * sub, w * lanes:(w + 1) * lanes]
            peak = jnp.max(jnp.maximum(jnp.abs(re), jnp.abs(im)), axis=0, keepdims=True)
            level = jnp.ceil(jnp.log2(jnp.maximum(peak, 1e-30)) * 4.0 + 0.01)
            factor = jnp.exp2(level * -0.25) * LEVELS
            top = jnp.round(re * factor).astype(jnp.int32)
            bottom = jnp.round(im * factor).astype(jnp.int32)
            codes[dest, pl.ds(w, sub, stride=local_wins), :] = top * 65536 + (bottom & 65535)
            codes[dest, pl.ds(sub * local_wins + w, 1), :] = level.astype(jnp.int32)

    def win_copy(hop):
        to = lax.rem(win + hop, wins)
        return pltpu.make_async_remote_copy(
            src_ref=codes.at[to], dst_ref=out_ref.at[sta, win],
            send_sem=ws_sem.at[hop], recv_sem=wr_sem.at[hop],
            device_id={"win": to}, device_id_type=MESH,
        )

    for hop in range(1, wins):
        win_copy(hop).start()
    keep = pltpu.make_async_copy(codes.at[win], out_ref.at[sta, win], own_sem)
    keep.start()
    keep.wait()

    def slot(block, j):
        return out_ref.at[block, lax.rem(win - j + wins, wins)]

    def right_copy(block, t, j):
        return pltpu.make_async_remote_copy(
            src_ref=slot(block, j), dst_ref=slot(block, j),
            send_sem=rs_sem.at[t, j], recv_sem=rr_sem.at[t, j],
            device_id={"sta": sta + 1}, device_id_type=MESH,
        )

    def left_copy(block, t, j):
        return pltpu.make_async_remote_copy(
            src_ref=slot(block, j), dst_ref=slot(block, j),
            send_sem=ls_sem.at[t, j], recv_sem=lr_sem.at[t, j],
            device_id={"sta": sta - 1}, device_id_type=MESH,
        )

    for j in range(wins):
        if j > 0:
            win_copy(j).wait_recv()

        @pl.when(has_right)
        def _(j=j):
            right_copy(sta, 0, j).start()

        @pl.when(has_left)
        def _(j=j):
            left_copy(sta, 0, j).start()

    def relay(t, carry):
        for j in range(wins):
            @pl.when(sta - t >= 0)
            def _(j=j):
                right_copy(sta - t, t - 1, j).wait_recv()

                @pl.when(has_right)
                def _():
                    right_copy(sta - t, t, j).start()

            @pl.when(sta + t < stas)
            def _(j=j):
                left_copy(sta + t, t - 1, j).wait_recv()

                @pl.when(has_left)
                def _():
                    left_copy(sta + t, t, j).start()
        return carry

    lax.fori_loop(1, stas, relay, 0)

    def drain(t, carry):
        for j in range(wins):
            @pl.when(has_right & (sta - t >= 0))
            def _(j=j):
                right_copy(sta - t, t, j).wait_send()

            @pl.when(has_left & (sta + t < stas))
            def _(j=j):
                left_copy(sta + t, t, j).wait_send()
        return carry

    lax.fori_loop(0, stas - 1, drain, 0)
    for hop in range(1, wins):
        win_copy(hop).wait_send()


def gathered_codes(x, table, local_wins):
    stas = lax.axis_size("sta")
    wins = lax.axis_size("win")
    cols = x.shape[0]
    lanes = cols // local_wins
    rows = BAND // wins * local_wins + 8
    dma = pltpu.SemaphoreType.DMA
    vmem = pl.BlockSpec(memory_space=pltpu.VMEM)
    return pl.pallas_call(
        functools.partial(spectra_kernel, stas, wins, local_wins),
        out_shape=jax.ShapeDtypeStruct((stas, wins, rows, lanes), jnp.int32),
        in_specs=[vmem, pl.BlockSpec(memory_space=pl.ANY)],
        out_specs=vmem,
        scratch_shapes=[
            pltpu.VMEM((4, 2, ROWS, PAD), jnp.bfloat16),
            pltpu.VMEM((cols, PAD), jnp.bfloat16),
            pltpu.VMEM((cols, PAD), jnp.bfloat16),
            pltpu.VMEM((2, ROWS, cols), jnp.float32),
            pltpu.VMEM((2, ROWS, cols), jnp.float32),
            pltpu.VMEM((2, ROWS, cols), jnp.float32),
            pltpu.VMEM((wins, rows, lanes), jnp.int32),
            dma((4,)), dma((2,)), dma((2,)), dma((wins,)), dma((wins,)),
            dma((stas, wins)), dma((stas, wins)), dma((stas, wins)), dma((stas, wins)), dma(()),
        ],
        compiler_params=pltpu.CompilerParams(
            collective_id=0, has_side_effects=True, vmem_limit_bytes=48 << 20
        ),
        name="spectra",
    )(x, table)


def pair_kernel(wins, local_wins, group, steps, slots_ref, left_ref, right_ref, out_ref):
    step = pl.program_id(1)
    lanes = left_ref.shape[-1]
    span = group * local_wins
    half = wins * span
    depth = 2 * half
    scale_row = left_ref.shape[2] - 8
    bins = out_ref.shape[1]
    factor = 1.0 / math.sqrt(wins * local_wins)

    def decoded(ref, first):
        planes = ([], [])
        for s in range(wins):
            word = ref[0, s, pl.ds(pl.multiple_of(first * local_wins, 8), span), :]
            odd = lax.broadcasted_iota(jnp.int32, (span, lanes), 0) % local_wins
            level = jnp.zeros((span, lanes), jnp.float32)
            for w in range(local_wins):
                unit = jnp.exp2(ref[0, s, scale_row + w:scale_row + w + 1, :].astype(jnp.float32) * 0.25)
                level = jnp.where(odd == w, unit * (1.0 / LEVELS), level)
            planes[0].append((word >> 16).astype(jnp.float32) * level)
            planes[1].append(((word << 16) >> 16).astype(jnp.float32) * level)
        return jnp.concatenate(planes[0], axis=0), jnp.concatenate(planes[1], axis=0)

    def turned(value):
        high = value.astype(jnp.bfloat16).astype(jnp.float32)
        both = jnp.concatenate([high, value - high], axis=0)
        return both.T.astype(jnp.bfloat16)

    row_bin = lax.broadcasted_iota(jnp.int32, (depth, 2 * lanes), 0) // local_wins % group
    col_odd = lax.broadcasted_iota(jnp.int32, (depth, 2 * lanes), 1) // lanes
    keep = row_bin % 2 == col_odd
    lane_pair = lax.broadcasted_iota(jnp.int32, (lanes, 2 * depth), 1) // local_wins % group // 2

    for g in range(bins // group):
        first = step * bins + g * group
        left_re, left_im = decoded(left_ref, first)
        right_re, right_im = decoded(right_ref, first)
        streams = (
            turned(jnp.concatenate([left_re, left_im], axis=0)),
            turned(jnp.concatenate([left_im, -left_re], axis=0)),
        )
        held = jnp.concatenate([right_re, right_im], axis=0)
        held = jnp.where(keep, jnp.concatenate([held, held], axis=1), 0.0)
        high, low = split(held)
        held = jnp.concatenate([high, high, low, low], axis=0)
        for m in range(group // 2):
            for p in range(2):
                part = jnp.where(lane_pair == m, streams[p], jnp.zeros_like(streams[p]))
                part = jnp.concatenate([part, part], axis=1)
                out = jnp.dot(part, held, preferred_element_type=jnp.float32) * factor
                out = out.astype(jnp.bfloat16)
                out_ref[0, g * group + 2 * m, p] = out[:, :lanes]
                out_ref[0, g * group + 2 * m + 1, p] = out[:, lanes:]


def pair_products(codes, slots, local_wins):
    stas, wins, rows, lanes = codes.shape
    bins = (rows - 8) // local_wins
    group = max(4, 64 // (2 * wins * local_wins))
    chunk = min(16, bins)
    count = slots.shape[0]
    spec = pltpu.PrefetchScalarGridSpec(
        num_scalar_prefetch=1,
        grid=(count, bins // chunk),
        in_specs=[
            pl.BlockSpec((1, wins, rows, lanes), lambda i, j, s: (s[i, 0], 0, 0, 0)),
            pl.BlockSpec((1, wins, rows, lanes), lambda i, j, s: (s[i, 1], 0, 0, 0)),
        ],
        out_specs=pl.BlockSpec((1, chunk, 2, lanes, lanes), lambda i, j, s: (i, j, 0, 0, 0)),
    )
    return pl.pallas_call(
        functools.partial(pair_kernel, wins, local_wins, group, bins // chunk),
        out_shape=jax.ShapeDtypeStruct((count, bins, 2, lanes, lanes), jnp.bfloat16),
        grid_spec=spec,
        compiler_params=pltpu.CompilerParams(vmem_limit_bytes=32 << 20),
        name="pairs",
    )(slots, codes, codes)


def local(table, records, valid_counts, pair_blocks):
    stations, local_wins, samples = records.shape
    freq = lax.axis_index("freq")
    index = freq * samples + jnp.arange(samples, dtype=jnp.int32)
    edge = SAMPLES // 20
    position = jnp.minimum(index, SAMPLES - 1 - index)
    ramp = 0.5 * (1.0 - jnp.cos(math.pi * (position.astype(jnp.float32) + 0.5) / edge))
    weight = jnp.where(position < edge, ramp, 1.0) / math.sqrt(SAMPLES)
    live = jnp.arange(stations, dtype=jnp.int32) < valid_counts[0]
    x = jnp.where(live[:, None, None], records * weight, 0.0)
    x = jnp.swapaxes(x, 0, 1).reshape(local_wins * stations, samples)
    x = jnp.pad(x, ((0, 0), (0, PAD - samples)))
    codes = gathered_codes(x, jnp.asarray(table), local_wins)
    slots = pair_blocks.shape[0] // lax.axis_size("sta")
    mine = lax.dynamic_slice_in_dim(pair_blocks, lax.axis_index("sta") * slots, slots, 0)
    return pair_products(codes, mine, local_wins)[:, None]


def solution(mesh):
    in_specs = (P(("group", "sta"), "win", "freq"), P(("group", "sta")), P("group", None))
    out_specs = P(("group", "sta"), "freq", "win", None, None, None)
    body = functools.partial(local, dft_table())
    return jax.shard_map(body, mesh=mesh, in_specs=in_specs, out_specs=out_specs, check_vma=False)
```

time: 176 us -> 46.2 us (0.26)
  matrix products: 77.6 us -> 0 us
  waiting for transfers between devices: 60.9 us -> 0 us
  Pallas kernels: 0 us -> 40 us
  between operations: 17.8 us -> 0.71 us
  blocking collectives: 11.3 us -> 0 us
  starting transfers between devices: 3.45 us -> 0 us
    dot_general x4 -> x0, matrix products: 77.6 us -> none  [the longest x1 30.8 us: cross_pair(): jnp.einsum('fpwqa,fwqb->fpab', stacked, right_block, precision=PRECISE)]
    all_gather x2 -> x0, waiting for transfers between devices: 58.5 us -> none  [the longest x1 42 us: local(): portion = lax.all_gather(held_block[None], 'sta', axis=0, tiled=True)]
    pallas_call x0 -> x2, Pallas kernels: none -> 40 us  [the longest x1 32.8 us: gathered_codes(): pl.pallas_call(functools.partial(spectra_kernel, stas, wins, local_wins),...]
    all_to_all x1 -> x0, blocking collectives: 11.3 us -> none  [local(): lax.all_to_all(whitened, 'win', split_axis=0, concat_axis=1, tiled=True)]
    ppermute x2 -> x0, starting transfers between devices: 3.41 us -> none  [the longest x1 2.12 us: padded_2(): before = lax.ppermute(last, axis, up)]
    transpose x0 -> x1, other arithmetic: none -> 3.04 us  [local(): x = jnp.swapaxes(x, 0, 1).reshape(local_wins * stations, samples)]
    transpose x0 -> x1, local copies, waits for them, and re-layouts: none -> 1.86 us  [local(): x = jnp.swapaxes(x, 0, 1).reshape(local_wins * stations, samples)]
  transfers between devices with their start and end apart: 4 -> 0, of which waited for: 3 -> 0; matrix products, arithmetic and copies ran while one was open for 0% -> 0% of each run, Pallas kernels for 0% -> 0%
where the time goes in v1:
time: 46.2 us; the launch traced here: 46 us
  Pallas kernels  40 us (87%)
  other arithmetic  3.11 us (7%)
  local copies, waits for them, and re-layouts  2.17 us (5%)
  between operations  0.71 us (2%)
    pallas_call x1, Pallas kernels, gathered_codes(): pl.pallas_call(functools.partial(spectra_kernel, stas, wins, local_wins),...  32.8 us
    pallas_call x1, Pallas kernels, pair_products(): pl.pallas_call(functools.partial(pair_kernel, wins, local_wins, group, bi...  7.22 us
    transpose x1, other arithmetic, local(): x = jnp.swapaxes(x, 0, 1).reshape(local_wins * stations, samples)  3.04 us
    transpose x1, local copies, waits for them, and re-layouts, local(): x = jnp.swapaxes(x, 0, 1).reshape(local_wins * stations, samples)  1.86 us

profile of v1, /device:TPU:0, one launch (start us, length us, event | category | flops | bytes accessed | tf_op | source)
XLA Modules:
  0.0 46.0 jit_solution(868191387870751196)
XLA Ops:
  0.0 0.0 copy-start
  0.7 0.0 copy-done
  0.7 0.1 constant_dynamic-slice_fusion
  0.8 0.1 copy.7.slots_ref
  0.9 0.1 select_multiply_fusion
  0.9 3.0 %select_bitcast_fusion = f32[2,128,1800]{1,2,0:T(8,128)} fusion(f32[128,2,1800]{0,2,1:T(8,128)} %param.4, f32[1800]{0:T(1024)S(1)} %select_multiply_fusion, pred[128]{0:T(512)(128)(4,1)S(1)} %iota_compare_fusion), kind=kLoop, calls=%fused_computation | loop fusion | flops 921600 | bytes 3693728 | tf_op jit(solution)/shard_map/transpose | solution.py:355
  4.0 1.9 %copy.6 = f32[2,128,1800]{2,1,0:T(8,128)S(1)} copy(f32[2,128,1800]{1,2,0:T(8,128)} %select_bitcast_fusion) | data formatting | bytes 3686400 | tf_op jit(solution)/shard_map/transpose | solution.py:355
  5.8 0.1 pad.4.x_ref
  6.0 32.8 %spectra.1.left_ref.right_ref = s32[4,2,264,128]{3,2,1,0:T(8,128)S(1)} custom-call(f32[256,1920]{1,0:T(8,128)S(1)} %pad.4.x_ref, bf16[2,2,2,272,1920]{4,3,2,1,0:T(8,128)(2,1)} %constant.37.clone.table_ref), custom_call_target="tpu_custom_call" | custom-call | tf_op jit(solution)/shard_map/spectra/pallas_call | solution.py:243
  38.8 7.2 %pairs.1 = bf16[1,128,2,128,128]{4,3,2,1,0:T(8,128)(2,1)} custom-call(s32[1,2]{1,0:T(1,128)S(1)} %copy.7.slots_ref, s32[4,2,264,128]{3,2,1,0:T(8,128)S(1)} %spectra.1.left_ref.right_ref, s32[4,2,264,128]{3,2,1,0:T(8,128)S(1)} %spectra.1.left_ref.right_ref), custom_call_target="tpu_custom_call" | custom-call | tf_op jit(solution)/shard_map/pairs/pallas_call | solution.py:336
  (1 shorter events, 0.0 us)
Async XLA Ops:
  0.0 0.7 %copy-start = (s32[4,2]{0,1:T(2,128)S(1)}, s32[4,2]{0,1:T(2,128)}, u32[]{:S(2)}) copy-start(s32[4,2]{0,1:T(2,128)} %param.6) | copy-start | bytes 100

commit v2 on v1

--- a/solution.py
+++ b/solution.py
@@ -33,7 +33,8 @@
     for band in range(2):
         phase = (band_bins(band)[:, None] + 1) * np.arange(half)[None] % SAMPLES
         angle = phase * (2.0 * math.pi / SAMPLES)
-        for part, value in enumerate((np.cos(angle), -np.sin(angle))):
+        for part, wave in enumerate((np.cos(angle), -np.sin(angle))):
+            value = wave / math.sqrt(SAMPLES)
             high = value.astype(jnp.bfloat16)
             table[band, part, 0, :, :half] = high
             table[band, part, 1, :, :half] = (value - high.astype(np.float64)).astype(jnp.bfloat16)
@@ -45,21 +46,20 @@
     return high, (value - high.astype(jnp.float32)).astype(jnp.bfloat16)
 
 
-def dot_nt(a, b):
-    return lax.dot_general(a, b, (((1,), (1,)), ((), ())), preferred_element_type=jnp.float32)
+def dot(a, b):
+    return jnp.dot(a, b, preferred_element_type=jnp.float32)
 
 
 def spectra_kernel(
-    stas, wins, local_wins, x_ref, table_ref, out_ref,
-    tab, xh, xl, give, got, own, codes,
-    tab_sem, fs_sem, fr_sem, ws_sem, wr_sem, rs_sem, rr_sem, ls_sem, lr_sem, own_sem,
+    stas, wins, local_wins, live_ref, x_ref, table_ref, out_ref,
+    tab, raw, xh, xl, give, got, own, codes,
+    tab_sem, raw_sem, fs_sem, fr_sem, ws_sem, wr_sem, rs_sem, rr_sem, ls_sem, lr_sem, own_sem,
 ):
     sta = lax.axis_index("sta")
     win = lax.axis_index("win")
     freq = lax.axis_index("freq")
     other = 1 - freq
-    cols = x_ref.shape[0]
-    lanes = cols // local_wins
+    samples, lanes = x_ref.shape[1:]
     sub = BAND // wins
     has_right = sta < stas - 1
     has_left = sta > 0
@@ -70,6 +70,8 @@
             table_ref.at[band, step % 2], tab.at[step], tab_sem.at[step]
         )
 
+    raw_copy = pltpu.make_async_copy(x_ref, raw, raw_sem)
+    raw_copy.start()
     for step in range(4):
         table_copy(step).start()
 
@@ -88,9 +90,23 @@
     def _():
         pl.semaphore_signal(barrier, inc=1, device_id={"sta": sta - 1}, device_id_type=MESH)
 
-    high, low = split(x_ref[...])
-    xh[...] = high
-    xl[...] = low
+    edge = SAMPLES // 20
+    span = -(-edge // 8) * 8
+    begin = pl.multiple_of(freq * (samples - span), 8)
+    at = begin + lax.broadcasted_iota(jnp.int32, (span, lanes), 0)
+    position = jnp.where(freq == 0, at, samples - 1 - at)
+    ramp = 0.5 * (1.0 - jnp.cos(math.pi * (position.astype(jnp.float32) + 0.5) / edge))
+    ramp = jnp.where(position < edge, ramp, 1.0)
+    raw_copy.wait()
+    for w in range(local_wins):
+        part = slice(w * lanes, (w + 1) * lanes)
+        raw[w, pl.ds(begin, span), :] = raw[w, pl.ds(begin, span), :] * ramp
+        high, low = split(raw[w])
+        xh[:samples, part] = high
+        xl[:samples, part] = low
+    blank = jnp.zeros((PAD - samples, local_wins * lanes), jnp.bfloat16)
+    xh[samples:] = blank
+    xl[samples:] = blank
 
     ends = jnp.where(has_right, 1, 0) + jnp.where(has_left, 1, 0)
     pl.semaphore_wait(barrier, wins + ends)
@@ -100,8 +116,8 @@
 
     def partial(step):
         table_copy(step).wait()
-        value = dot_nt(tab[step, 0], xh[...]) + (
-            dot_nt(tab[step, 0], xl[...]) + dot_nt(tab[step, 1], xh[...])
+        value = dot(tab[step, 0], xh[...]) + (
+            dot(tab[step, 0], xl[...]) + dot(tab[step, 1], xh[...])
         )
         return value * sign
 
@@ -136,7 +152,9 @@
     counted = (
         jnp.minimum(bin_at + HALF_WIDTH, BINS - 1) - jnp.maximum(bin_at - HALF_WIDTH, 0) + 1
     ).astype(jnp.float32)
-    inverse = 1.0 / jnp.maximum(summed / counted, AMP_FLOOR)
+    station = lax.broadcasted_iota(jnp.int32, (1, local_wins * lanes), 1) % lanes
+    live = (station < live_ref[0]).astype(jnp.float32)
+    inverse = live / jnp.maximum(summed / counted, AMP_FLOOR)
     real = real[:BAND] * inverse
     imag = imag[:BAND] * inverse
 
@@ -232,35 +250,36 @@
         win_copy(hop).wait_send()
 
 
-def gathered_codes(x, table, local_wins):
+def gathered_codes(live, x, table):
     stas = lax.axis_size("sta")
     wins = lax.axis_size("win")
-    cols = x.shape[0]
-    lanes = cols // local_wins
+    local_wins, samples, lanes = x.shape
+    cols = local_wins * lanes
     rows = BAND // wins * local_wins + 8
     dma = pltpu.SemaphoreType.DMA
-    vmem = pl.BlockSpec(memory_space=pltpu.VMEM)
+    hold = pl.BlockSpec(memory_space=pl.ANY)
     return pl.pallas_call(
         functools.partial(spectra_kernel, stas, wins, local_wins),
         out_shape=jax.ShapeDtypeStruct((stas, wins, rows, lanes), jnp.int32),
-        in_specs=[vmem, pl.BlockSpec(memory_space=pl.ANY)],
-        out_specs=vmem,
+        in_specs=[pl.BlockSpec(memory_space=pltpu.SMEM), hold, hold],
+        out_specs=pl.BlockSpec(memory_space=pltpu.VMEM),
         scratch_shapes=[
             pltpu.VMEM((4, 2, ROWS, PAD), jnp.bfloat16),
-            pltpu.VMEM((cols, PAD), jnp.bfloat16),
-            pltpu.VMEM((cols, PAD), jnp.bfloat16),
+            pltpu.VMEM((local_wins, samples, lanes), jnp.float32),
+            pltpu.VMEM((PAD, cols), jnp.bfloat16),
+            pltpu.VMEM((PAD, cols), jnp.bfloat16),
             pltpu.VMEM((2, ROWS, cols), jnp.float32),
             pltpu.VMEM((2, ROWS, cols), jnp.float32),
             pltpu.VMEM((2, ROWS, cols), jnp.float32),
             pltpu.VMEM((wins, rows, lanes), jnp.int32),
-            dma((4,)), dma((2,)), dma((2,)), dma((wins,)), dma((wins,)),
+            dma((4,)), dma(()), dma((2,)), dma((2,)), dma((wins,)), dma((wins,)),
             dma((stas, wins)), dma((stas, wins)), dma((stas, wins)), dma((stas, wins)), dma(()),
         ],
         compiler_params=pltpu.CompilerParams(
-            collective_id=0, has_side_effects=True, vmem_limit_bytes=48 << 20
+            collective_id=0, has_side_effects=True, vmem_limit_bytes=61 << 20
         ),
         name="spectra",
-    )(x, table)
+    )(live, x, table)
 
 
 def pair_kernel(wins, local_wins, group, steps, slots_ref, left_ref, right_ref, out_ref):
@@ -273,15 +292,26 @@
     bins = out_ref.shape[1]
     factor = 1.0 / math.sqrt(wins * local_wins)
 
-    def decoded(ref, first):
+    odd = lax.broadcasted_iota(jnp.int32, (span, lanes), 0) % local_wins
+
+    def levels(ref, scale):
+        found = []
+        for s in range(wins):
+            level = jnp.zeros((span, lanes), jnp.float32)
+            for w in range(local_wins):
+                row = ref[0, s, scale_row + w:scale_row + w + 1, :].astype(jnp.float32)
+                level = jnp.where(odd == w, jnp.exp2(row * 0.25) * scale, level)
+            found.append(level)
+        return found
+
+    left_levels = levels(left_ref, 1.0 / LEVELS)
+    right_levels = levels(right_ref, factor / LEVELS)
+
+    def decoded(ref, first, found):
         planes = ([], [])
         for s in range(wins):
             word = ref[0, s, pl.ds(pl.multiple_of(first * local_wins, 8), span), :]
-            odd = lax.broadcasted_iota(jnp.int32, (span, lanes), 0) % local_wins
-            level = jnp.zeros((span, lanes), jnp.float32)
-            for w in range(local_wins):
-                unit = jnp.exp2(ref[0, s, scale_row + w:scale_row + w + 1, :].astype(jnp.float32) * 0.25)
-                level = jnp.where(odd == w, unit * (1.0 / LEVELS), level)
+            level = found[s]
             planes[0].append((word >> 16).astype(jnp.float32) * level)
             planes[1].append(((word << 16) >> 16).astype(jnp.float32) * level)
         return jnp.concatenate(planes[0], axis=0), jnp.concatenate(planes[1], axis=0)
@@ -298,8 +328,8 @@
 
     for g in range(bins // group):
         first = step * bins + g * group
-        left_re, left_im = decoded(left_ref, first)
-        right_re, right_im = decoded(right_ref, first)
+        left_re, left_im = decoded(left_ref, first, left_levels)
+        right_re, right_im = decoded(right_ref, first, right_levels)
         streams = (
             turned(jnp.concatenate([left_re, left_im], axis=0)),
             turned(jnp.concatenate([left_im, -left_re], axis=0)),
@@ -312,7 +342,7 @@
             for p in range(2):
                 part = jnp.where(lane_pair == m, streams[p], jnp.zeros_like(streams[p]))
                 part = jnp.concatenate([part, part], axis=1)
-                out = jnp.dot(part, held, preferred_element_type=jnp.float32) * factor
+                out = jnp.dot(part, held, preferred_element_type=jnp.float32)
                 out = out.astype(jnp.bfloat16)
                 out_ref[0, g * group + 2 * m, p] = out[:, :lanes]
                 out_ref[0, g * group + 2 * m + 1, p] = out[:, lanes:]
@@ -322,7 +352,7 @@
     stas, wins, rows, lanes = codes.shape
     bins = (rows - 8) // local_wins
     group = max(4, 64 // (2 * wins * local_wins))
-    chunk = min(16, bins)
+    chunk = min(32, bins)
     count = slots.shape[0]
     spec = pltpu.PrefetchScalarGridSpec(
         num_scalar_prefetch=1,
@@ -343,18 +373,8 @@
 
 
 def local(table, records, valid_counts, pair_blocks):
-    stations, local_wins, samples = records.shape
-    freq = lax.axis_index("freq")
-    index = freq * samples + jnp.arange(samples, dtype=jnp.int32)
-    edge = SAMPLES // 20
-    position = jnp.minimum(index, SAMPLES - 1 - index)
-    ramp = 0.5 * (1.0 - jnp.cos(math.pi * (position.astype(jnp.float32) + 0.5) / edge))
-    weight = jnp.where(position < edge, ramp, 1.0) / math.sqrt(SAMPLES)
-    live = jnp.arange(stations, dtype=jnp.int32) < valid_counts[0]
-    x = jnp.where(live[:, None, None], records * weight, 0.0)
-    x = jnp.swapaxes(x, 0, 1).reshape(local_wins * stations, samples)
-    x = jnp.pad(x, ((0, 0), (0, PAD - samples)))
-    codes = gathered_codes(x, jnp.asarray(table), local_wins)
+    local_wins = records.shape[1]
+    codes = gathered_codes(valid_counts, jnp.transpose(records, (1, 2, 0)), jnp.asarray(table))
     slots = pair_blocks.shape[0] // lax.axis_size("sta")
     mine = lax.dynamic_slice_in_dim(pair_blocks, lax.axis_index("sta") * slots, slots, 0)
     return pair_products(codes, mine, local_wins)[:, None]

time: 46.2 us -> 42.2 us (0.913)
  other arithmetic: 3.11 us -> 0 us
  local copies, waits for them, and re-layouts: 2.17 us -> 1.41 us
    transpose x1 -> x0, other arithmetic: 3.04 us -> none  [local(): x = jnp.swapaxes(x, 0, 1).reshape(local_wins * stations, samples)]
    transpose x1 -> x0, local copies, waits for them, and re-layouts: 1.86 us -> none  [local(): x = jnp.swapaxes(x, 0, 1).reshape(local_wins * stations, samples)]
    pallas_call x1, Pallas kernels: 7.22 us -> 5.67 us  [pair_products(): pl.pallas_call(functools.partial(pair_kernel, wins, local_wins, group, bi...]
    pallas_call x1, Pallas kernels: 32.8 us -> 34.2 us  [gathered_codes(): pl.pallas_call(functools.partial(spectra_kernel, stas, wins, local_wins),...]
    unnamed x3 -> x5, local copies, waits for them, and re-layouts: 0.1 us -> 1.34 us
where the time goes in v2:
time: 42.2 us; the launch traced here: 42 us
  Pallas kernels  39.9 us (95%)
  local copies, waits for them, and re-layouts  1.41 us (3%)
  between operations  0.69 us (2%)
    pallas_call x1, Pallas kernels, gathered_codes(): pl.pallas_call(functools.partial(spectra_kernel, stas, wins, local_wins),...  34.2 us
    pallas_call x1, Pallas kernels, pair_products(): pl.pallas_call(functools.partial(pair_kernel, wins, local_wins, group, bi...  5.67 us
    unnamed x5, local copies, waits for them, and re-layouts  1.34 us

profile of v2, /device:TPU:0, one launch (start us, length us, event | category | flops | bytes accessed | tf_op | source)
XLA Modules:
  0.0 42.0 jit_solution(4789645160432480935)
XLA Ops:
  0.0 0.0 copy-start
  0.7 0.0 copy-done
  0.7 0.1 constant_dynamic-slice_fusion
  0.8 0.1 copy.6.slots_ref
  0.8 34.2 %spectra.1.left_ref.right_ref = s32[4,2,264,128]{3,2,1,0:T(8,128)} custom-call(s32[1]{0:T(128)S(6)} %copy.7.live_ref, f32[2,1800,128]{2,1,0:T(8,128)} %bitcast.2, bf16[2,2,2,272,1920]{4,3,2,1,0:T(8,128)(2,1)} %constant.11.clone.table_ref), custom_call_target="tpu_custom_call" | custom-call | tf_op jit(solution)/shard_map/spectra/pallas_call | solution.py:261
  35.1 0.0 copy-start.1
  35.1 1.2 %copy-done.1 = s32[4,2,264,128]{3,2,1,0:T(8,128)S(1)} copy-done((s32[4,2,264,128]{3,2,1,0:T(8,128)S(1)}, s32[4,2,264,128]{3,2,1,0:T(8,128)}, u32[]{:S(2)}) %copy-start.1) | copy-done | bytes 1081368
  36.3 5.7 %pairs.1 = bf16[1,128,2,128,128]{4,3,2,1,0:T(8,128)(2,1)} custom-call(s32[1,2]{1,0:T(1,128)S(1)} %copy.6.slots_ref, s32[4,2,264,128]{3,2,1,0:T(8,128)S(1)} %copy-done.1, s32[4,2,264,128]{3,2,1,0:T(8,128)S(1)} %copy-done.1), custom_call_target="tpu_custom_call" | custom-call | tf_op jit(solution)/shard_map/pairs/pallas_call | solution.py:366
Async XLA Ops:
  0.0 0.7 %copy-start = (s32[4,2]{0,1:T(2,128)S(1)}, s32[4,2]{0,1:T(2,128)}, u32[]{:S(2)}) copy-start(s32[4,2]{0,1:T(2,128)} %param.6) | copy-start | bytes 100
  35.1 1.2 %copy-start.1 = (s32[4,2,264,128]{3,2,1,0:T(8,128)S(1)}, s32[4,2,264,128]{3,2,1,0:T(8,128)}, u32[]{:S(2)}) copy-start(s32[4,2,264,128]{3,2,1,0:T(8,128)} %spectra.1.left_ref.right_ref) | copy-start | bytes 3244036

commit v3 on v2

--- a/solution.py
+++ b/solution.py
@@ -21,23 +21,18 @@
 MESH = pl.DeviceIdType.MESH
 
 
-def band_bins(band):
-    own = np.arange(BAND) + band * BAND
-    halo = np.arange(HALO) + (BAND if band == 0 else BAND - HALO)
-    return np.concatenate([own, halo])
-
-
 def dft_table():
     half = SAMPLES // 2
     table = np.zeros((2, 2, 2, ROWS, PAD), jnp.bfloat16)
     for band in range(2):
-        phase = (band_bins(band)[:, None] + 1) * np.arange(half)[None] % SAMPLES
+        bins = np.arange(ROWS) + band * (BAND - HALO)
+        phase = (bins[:, None] + 1) * np.arange(half)[None] % SAMPLES
         angle = phase * (2.0 * math.pi / SAMPLES)
         for part, wave in enumerate((np.cos(angle), -np.sin(angle))):
             value = wave / math.sqrt(SAMPLES)
             high = value.astype(jnp.bfloat16)
-            table[band, part, 0, :, :half] = high
-            table[band, part, 1, :, :half] = (value - high.astype(np.float64)).astype(jnp.bfloat16)
+            table[band, 0, part, :, :half] = high
+            table[band, 1, part, :, :half] = (value - high.astype(np.float64)).astype(jnp.bfloat16)
     return table
 
 
@@ -50,30 +45,45 @@
     return jnp.dot(a, b, preferred_element_type=jnp.float32)
 
 
+def chunk_rows(wins):
+    first = BAND // 2 + 2 * HALO if wins == 2 else ROWS
+    return (first, ROWS - first) if first < ROWS else (first,)
+
+
 def spectra_kernel(
     stas, wins, local_wins, live_ref, x_ref, table_ref, out_ref,
-    tab, raw, xh, xl, give, got, own, codes,
-    tab_sem, raw_sem, fs_sem, fr_sem, ws_sem, wr_sem, rs_sem, rr_sem, ls_sem, lr_sem, own_sem,
+    raw, xh, xl, spec, mag, codes,
+    raw_sem, tab_sem, fs_sem, fr_sem, ws_sem, wr_sem, rs_sem, rr_sem, ls_sem, lr_sem, own_sem,
+    *chunks,
 ):
     sta = lax.axis_index("sta")
     win = lax.axis_index("win")
     freq = lax.axis_index("freq")
     other = 1 - freq
     samples, lanes = x_ref.shape[1:]
+    cols = local_wins * lanes
     sub = BAND // wins
     has_right = sta < stas - 1
     has_left = sta > 0
-
-    def table_copy(step):
-        band = other if step < 2 else freq
+    sizes = chunk_rows(wins)
+    if len(sizes) == 2:
+        starts = (win * sizes[1], (1 - win) * sizes[0])
+    else:
+        starts = (0,)
+    tabs, gives, gots = chunks[0::3], chunks[1::3], chunks[2::3]
+
+    def table_copy(c, mine):
+        rows = pl.ds(pl.multiple_of(starts[c], 16), sizes[c])
         return pltpu.make_async_copy(
-            table_ref.at[band, step % 2], tab.at[step], tab_sem.at[step]
+            table_ref.at[freq if mine else other, :, :, rows, :], tabs[c].at[mine],
+            tab_sem.at[c, mine],
         )
 
     raw_copy = pltpu.make_async_copy(x_ref, raw, raw_sem)
     raw_copy.start()
-    for step in range(4):
-        table_copy(step).start()
+    for c in range(len(sizes)):
+        for mine in range(2):
+            table_copy(c, mine).start()
 
     barrier = pltpu.get_barrier_semaphore()
     pl.semaphore_signal(barrier, inc=1, device_id={"freq": other}, device_id_type=MESH)
@@ -104,119 +114,109 @@
         high, low = split(raw[w])
         xh[:samples, part] = high
         xl[:samples, part] = low
-    blank = jnp.zeros((PAD - samples, local_wins * lanes), jnp.bfloat16)
+    blank = jnp.zeros((PAD - samples, cols), jnp.bfloat16)
     xh[samples:] = blank
     xl[samples:] = blank
 
     ends = jnp.where(has_right, 1, 0) + jnp.where(has_left, 1, 0)
     pl.semaphore_wait(barrier, wins + ends)
 
-    odd = lax.broadcasted_iota(jnp.int32, (ROWS, 1), 0) % 2
-    sign = jnp.where((odd == 0) & (freq == 1), -1.0, 1.0).astype(jnp.float32)
-
-    def partial(step):
-        table_copy(step).wait()
-        value = dot(tab[step, 0], xh[...]) + (
-            dot(tab[step, 0], xl[...]) + dot(tab[step, 1], xh[...])
-        )
-        return value * sign
-
-    def freq_copy(step):
+    def partial(c, mine):
+        rows = sizes[c]
+        table_copy(c, mine).wait()
+        odd = lax.broadcasted_iota(jnp.int32, (2 * rows, 1), 0) % 2
+        sign = jnp.where((odd == 0) & (freq == 1), -1.0, 1.0).astype(jnp.float32)
+        both = dot(tabs[c][mine].reshape(4 * rows, PAD), xh[...])
+        rest = dot(tabs[c][mine, 0].reshape(2 * rows, PAD), xl[...])
+        value = (both[:2 * rows] + (both[2 * rows:] + rest)) * sign
+        return value.reshape(2, rows, cols)
+
+    def freq_copy(c):
         return pltpu.make_async_remote_copy(
-            src_ref=give.at[step], dst_ref=got.at[step],
-            send_sem=fs_sem.at[step], recv_sem=fr_sem.at[step],
+            src_ref=gives[c], dst_ref=gots[c],
+            send_sem=fs_sem.at[c], recv_sem=fr_sem.at[c],
             device_id={"freq": other}, device_id_type=MESH,
         )
 
-    for step in range(2):
-        give[step] = partial(step)
-        freq_copy(step).start()
-    for step in range(2):
-        own[step] = partial(2 + step)
-    for step in range(2):
-        freq_copy(step).wait()
-
-    real = own[0] + got[0]
-    imag = own[1] + got[1]
-    magnitude = jnp.sqrt(real * real + imag * imag)
-    row = lax.broadcasted_iota(jnp.int32, (BAND, ROWS), 0)
-    col = lax.broadcasted_iota(jnp.int32, (BAND, ROWS), 1)
-    place = jnp.where(col < BAND, col, jnp.where(freq == 0, col, col - BAND - HALO))
-    box = ((place - row <= HALF_WIDTH) & (row - place <= HALF_WIDTH)).astype(jnp.float32)
-    box = box.astype(jnp.bfloat16)
-    mag_high, mag_low = split(magnitude)
-    summed = jnp.dot(box, mag_high, preferred_element_type=jnp.float32) + jnp.dot(
-        box, mag_low, preferred_element_type=jnp.float32
-    )
-    bin_at = freq * BAND + lax.broadcasted_iota(jnp.int32, (BAND, 1), 0)
-    counted = (
-        jnp.minimum(bin_at + HALF_WIDTH, BINS - 1) - jnp.maximum(bin_at - HALF_WIDTH, 0) + 1
-    ).astype(jnp.float32)
-    station = lax.broadcasted_iota(jnp.int32, (1, local_wins * lanes), 1) % lanes
+    def transform(c, between=None):
+        rows = pl.ds(pl.multiple_of(starts[c], 16), sizes[c])
+        gives[c][...] = partial(c, 0)
+        freq_copy(c).start()
+        value = partial(c, 1)
+        if between is not None:
+            between()
+        freq_copy(c).wait_recv()
+        value = value + gots[c][...]
+        spec[:, rows, :] = value
+        mag[rows, :] = jnp.sqrt(value[0] * value[0] + value[1] * value[1])
+
+    station = lax.broadcasted_iota(jnp.int32, (1, cols), 1) % lanes
     live = (station < live_ref[0]).astype(jnp.float32)
-    inverse = live / jnp.maximum(summed / counted, AMP_FLOOR)
-    real = real[:BAND] * inverse
-    imag = imag[:BAND] * inverse
-
-    for dest in range(wins):
+
+    def encode(hop, start, count):
+        dest = lax.rem(win + hop, wins)
+        bin_at = freq * BAND + dest * sub + lax.broadcasted_iota(jnp.int32, (sub, count), 0)
+        near = start + freq * (BAND - HALO) + lax.broadcasted_iota(jnp.int32, (sub, count), 1)
+        box = (near - bin_at <= HALF_WIDTH) & (bin_at - near <= HALF_WIDTH)
+        box = box.astype(jnp.float32).astype(jnp.bfloat16)
+        high, low = split(mag[pl.ds(pl.multiple_of(start, 16), count), :])
+        summed = dot(box, high) + dot(box, low)
+        bin_at = freq * BAND + dest * sub + lax.broadcasted_iota(jnp.int32, (sub, 1), 0)
+        counted = (
+            jnp.minimum(bin_at + HALF_WIDTH, BINS - 1) - jnp.maximum(bin_at - HALF_WIDTH, 0) + 1
+        ).astype(jnp.float32)
+        inverse = live / jnp.maximum(summed / counted, AMP_FLOOR)
+        rows = pl.ds(pl.multiple_of(freq * HALO + dest * sub, 16), sub)
+        real = spec[0, rows, :] * inverse
+        imag = spec[1, rows, :] * inverse
         for w in range(local_wins):
-            re = real[dest * sub:(dest + 1) * sub, w * lanes:(w + 1) * lanes]
-            im = imag[dest * sub:(dest + 1) * sub, w * lanes:(w + 1) * lanes]
+            re = real[:, w * lanes:(w + 1) * lanes]
+            im = imag[:, w * lanes:(w + 1) * lanes]
             peak = jnp.max(jnp.maximum(jnp.abs(re), jnp.abs(im)), axis=0, keepdims=True)
             level = jnp.ceil(jnp.log2(jnp.maximum(peak, 1e-30)) * 4.0 + 0.01)
             factor = jnp.exp2(level * -0.25) * LEVELS
             top = jnp.round(re * factor).astype(jnp.int32)
             bottom = jnp.round(im * factor).astype(jnp.int32)
-            codes[dest, pl.ds(w, sub, stride=local_wins), :] = top * 65536 + (bottom & 65535)
-            codes[dest, pl.ds(sub * local_wins + w, 1), :] = level.astype(jnp.int32)
+            codes[hop, pl.ds(w, sub, stride=local_wins), :] = top * 65536 + (bottom & 65535)
+            codes[hop, pl.ds(sub * local_wins + w, 1), :] = level.astype(jnp.int32)
 
     def win_copy(hop):
-        to = lax.rem(win + hop, wins)
         return pltpu.make_async_remote_copy(
-            src_ref=codes.at[to], dst_ref=out_ref.at[sta, win],
+            src_ref=codes.at[hop], dst_ref=out_ref.at[sta, win],
             send_sem=ws_sem.at[hop], recv_sem=wr_sem.at[hop],
-            device_id={"win": to}, device_id_type=MESH,
-        )
-
-    for hop in range(1, wins):
-        win_copy(hop).start()
-    keep = pltpu.make_async_copy(codes.at[win], out_ref.at[sta, win], own_sem)
-    keep.start()
-    keep.wait()
+            device_id={"win": lax.rem(win + hop, wins)}, device_id_type=MESH,
+        )
 
     def slot(block, j):
         return out_ref.at[block, lax.rem(win - j + wins, wins)]
 
-    def right_copy(block, t, j):
+    def right_copy(block, t, j, own=False):
         return pltpu.make_async_remote_copy(
-            src_ref=slot(block, j), dst_ref=slot(block, j),
+            src_ref=codes.at[0] if own else slot(block, j), dst_ref=slot(block, j),
             send_sem=rs_sem.at[t, j], recv_sem=rr_sem.at[t, j],
             device_id={"sta": sta + 1}, device_id_type=MESH,
         )
 
-    def left_copy(block, t, j):
+    def left_copy(block, t, j, own=False):
         return pltpu.make_async_remote_copy(
-            src_ref=slot(block, j), dst_ref=slot(block, j),
+            src_ref=codes.at[0] if own else slot(block, j), dst_ref=slot(block, j),
             send_sem=ls_sem.at[t, j], recv_sem=lr_sem.at[t, j],
             device_id={"sta": sta - 1}, device_id_type=MESH,
         )
 
-    for j in range(wins):
-        if j > 0:
-            win_copy(j).wait_recv()
-
+    def depart(j):
         @pl.when(has_right)
-        def _(j=j):
-            right_copy(sta, 0, j).start()
+        def _():
+            right_copy(sta, 0, j, j == 0).start()
 
         @pl.when(has_left)
-        def _(j=j):
-            left_copy(sta, 0, j).start()
-
-    def relay(t, carry):
-        for j in range(wins):
+        def _():
+            left_copy(sta, 0, j, j == 0).start()
+
+    def relay(low, high, j):
+        def step(t, carry):
             @pl.when(sta - t >= 0)
-            def _(j=j):
+            def _():
                 right_copy(sta - t, t - 1, j).wait_recv()
 
                 @pl.when(has_right)
@@ -224,15 +224,38 @@
                     right_copy(sta - t, t, j).start()
 
             @pl.when(sta + t < stas)
-            def _(j=j):
+            def _():
                 left_copy(sta + t, t - 1, j).wait_recv()
 
                 @pl.when(has_left)
                 def _():
                     left_copy(sta + t, t, j).start()
-        return carry
-
-    lax.fori_loop(1, stas, relay, 0)
+
+            return carry
+
+        lax.fori_loop(low, high, step, 0)
+
+    transform(0)
+    encode(0, starts[0], sizes[0])
+    depart(0)
+    keep = pltpu.make_async_copy(codes.at[0], out_ref.at[sta, win], own_sem)
+    keep.start()
+    early = min(2, stas)
+    if len(sizes) == 2:
+        transform(1, lambda: relay(1, early, 0))
+    for hop in range(1, wins):
+        encode(hop, 0, ROWS)
+        win_copy(hop).start()
+    if len(sizes) == 1:
+        relay(1, early, 0)
+    late = min(3, stas)
+    relay(early, late, 0)
+    for j in range(1, wins):
+        win_copy(j).wait_recv()
+        depart(j)
+    relay(late, stas, 0)
+    for j in range(1, wins):
+        relay(1, stas, j)
 
     def drain(t, carry):
         for j in range(wins):
@@ -246,8 +269,11 @@
         return carry
 
     lax.fori_loop(0, stas - 1, drain, 0)
+    for c in range(len(sizes)):
+        freq_copy(c).wait_send()
     for hop in range(1, wins):
         win_copy(hop).wait_send()
+    keep.wait()
 
 
 def gathered_codes(live, x, table):
@@ -257,6 +283,10 @@
     cols = local_wins * lanes
     rows = BAND // wins * local_wins + 8
     dma = pltpu.SemaphoreType.DMA
+    chunks = []
+    for size in chunk_rows(wins):
+        chunks.append(pltpu.VMEM((2, 2, 2, size, PAD), jnp.bfloat16))
+        chunks += [pltpu.VMEM((2, size, cols), jnp.float32)] * 2
     hold = pl.BlockSpec(memory_space=pl.ANY)
     return pl.pallas_call(
         functools.partial(spectra_kernel, stas, wins, local_wins),
@@ -264,19 +294,17 @@
         in_specs=[pl.BlockSpec(memory_space=pltpu.SMEM), hold, hold],
         out_specs=pl.BlockSpec(memory_space=pltpu.VMEM),
         scratch_shapes=[
-            pltpu.VMEM((4, 2, ROWS, PAD), jnp.bfloat16),
             pltpu.VMEM((local_wins, samples, lanes), jnp.float32),
             pltpu.VMEM((PAD, cols), jnp.bfloat16),
             pltpu.VMEM((PAD, cols), jnp.bfloat16),
             pltpu.VMEM((2, ROWS, cols), jnp.float32),
-            pltpu.VMEM((2, ROWS, cols), jnp.float32),
-            pltpu.VMEM((2, ROWS, cols), jnp.float32),
+            pltpu.VMEM((ROWS, cols), jnp.float32),
             pltpu.VMEM((wins, rows, lanes), jnp.int32),
-            dma((4,)), dma(()), dma((2,)), dma((2,)), dma((wins,)), dma((wins,)),
+            dma(()), dma((2, 2)), dma((2,)), dma((2,)), dma((wins,)), dma((wins,)),
             dma((stas, wins)), dma((stas, wins)), dma((stas, wins)), dma((stas, wins)), dma(()),
-        ],
+        ] + chunks,
         compiler_params=pltpu.CompilerParams(
-            collective_id=0, has_side_effects=True, vmem_limit_bytes=61 << 20
+            collective_id=0, has_side_effects=True, vmem_limit_bytes=62 << 20
         ),
         name="spectra",
     )(live, x, table)
@@ -367,7 +395,7 @@
         functools.partial(pair_kernel, wins, local_wins, group, bins // chunk),
         out_shape=jax.ShapeDtypeStruct((count, bins, 2, lanes, lanes), jnp.bfloat16),
         grid_spec=spec,
-        compiler_params=pltpu.CompilerParams(vmem_limit_bytes=32 << 20),
+        compiler_params=pltpu.CompilerParams(vmem_limit_bytes=62 << 20),
         name="pairs",
     )(slots, codes, codes)
 

time: 42.2 us -> 43.6 us (1.033)
  Pallas kernels: 39.9 us -> 42 us
  local copies, waits for them, and re-layouts: 1.41 us -> 0.75 us
    pallas_call x1, Pallas kernels: 5.67 us -> 6.85 us  [pair_products(): pl.pallas_call(functools.partial(pair_kernel, wins, local_wins, group, bi...]
    pallas_call x1, Pallas kernels: 34.2 us -> 35.2 us  [gathered_codes(): pl.pallas_call(functools.partial(spectra_kernel, stas, wins, local_wins),...]
    unnamed x5 -> x3, local copies, waits for them, and re-layouts: 1.34 us -> 0.68 us
where the time goes in v3:
time: 43.6 us; the launch traced here: 43.4 us
  Pallas kernels  42 us (96%)
  local copies, waits for them, and re-layouts  0.75 us (2%)
  between operations  0.68 us (2%)
    pallas_call x1, Pallas kernels, gathered_codes(): pl.pallas_call(functools.partial(spectra_kernel, stas, wins, local_wins),...  35.2 us
    pallas_call x1, Pallas kernels, pair_products(): pl.pallas_call(functools.partial(pair_kernel, wins, local_wins, group, bi...  6.85 us

profile of v3, /device:TPU:0, one launch (start us, length us, event | category | flops | bytes accessed | tf_op | source)
XLA Modules:
  0.0 43.4 jit_solution(4458159739945338184)
XLA Ops:
  0.0 0.0 copy-start
  0.7 0.0 copy-done
  0.7 0.1 constant_dynamic-slice_fusion
  0.8 0.7 %copy.6.slots_ref = s32[1,2]{1,0:T(1,128)} copy(s32[1,2]{0,1:T(2,128)S(1)} %constant_dynamic-slice_fusion) | data formatting | bytes 16
  1.4 35.2 %spectra.1.left_ref.right_ref = s32[4,2,264,128]{3,2,1,0:T(8,128)} custom-call(s32[1]{0:T(128)S(6)} %copy.7.live_ref, f32[2,1800,128]{2,1,0:T(8,128)} %bitcast.2, bf16[2,2,2,272,1920]{4,3,2,1,0:T(8,128)(2,1)} %constant.11.clone.table_ref), custom_call_target="tpu_custom_call" | custom-call | tf_op jit(solution)/shard_map/spectra/pallas_call | solution.py:291
  36.6 6.9 %pairs.1 = bf16[1,128,2,128,128]{4,3,2,1,0:T(8,128)(2,1)} custom-call(s32[1,2]{1,0:T(1,128)} %copy.6.slots_ref, s32[4,2,264,128]{3,2,1,0:T(8,128)} %spectra.1.left_ref.right_ref, s32[4,2,264,128]{3,2,1,0:T(8,128)} %spectra.1.left_ref.right_ref), custom_call_target="tpu_custom_call" | custom-call | tf_op jit(solution)/shard_map/pairs/pallas_call | solution.py:394
Async XLA Ops:
  0.0 0.7 %copy-start = (s32[4,2]{0,1:T(2,128)S(1)}, s32[4,2]{0,1:T(2,128)}, u32[]{:S(2)}) copy-start(s32[4,2]{0,1:T(2,128)} %param.6) | copy-start | bytes 100

commit v4 on v3

--- a/solution.py
+++ b/solution.py
@@ -21,18 +21,16 @@
 MESH = pl.DeviceIdType.MESH
 
 
-def dft_table():
-    half = SAMPLES // 2
-    table = np.zeros((2, 2, 2, ROWS, PAD), jnp.bfloat16)
+def dft_factors():
+    table = np.zeros((2, 2, 2, ROWS, 128), np.float32)
     for band in range(2):
-        bins = np.arange(ROWS) + band * (BAND - HALO)
-        phase = (bins[:, None] + 1) * np.arange(half)[None] % SAMPLES
-        angle = phase * (2.0 * math.pi / SAMPLES)
-        for part, wave in enumerate((np.cos(angle), -np.sin(angle))):
-            value = wave / math.sqrt(SAMPLES)
-            high = value.astype(jnp.bfloat16)
-            table[band, 0, part, :, :half] = high
-            table[band, 1, part, :, :half] = (value - high.astype(np.float64)).astype(jnp.bfloat16)
+        bins = np.arange(ROWS)[:, None] + band * (BAND - HALO) + 1
+        base = bins * np.arange(128)[None] % SAMPLES * (2.0 * math.pi / SAMPLES)
+        turn = bins * 128 * np.arange(128)[None] % SAMPLES * (2.0 * math.pi / SAMPLES)
+        table[band, 0, 0] = np.cos(base) / math.sqrt(SAMPLES)
+        table[band, 0, 1] = -np.sin(base) / math.sqrt(SAMPLES)
+        table[band, 1, 0] = np.cos(turn)
+        table[band, 1, 1] = np.sin(turn)
     return table
 
 
@@ -53,7 +51,7 @@
 def spectra_kernel(
     stas, wins, local_wins, live_ref, x_ref, table_ref, out_ref,
     raw, xh, xl, spec, mag, codes,
-    raw_sem, tab_sem, fs_sem, fr_sem, ws_sem, wr_sem, rs_sem, rr_sem, ls_sem, lr_sem, own_sem,
+    raw_sem, fs_sem, fr_sem, ws_sem, wr_sem, rs_sem, rr_sem, ls_sem, lr_sem, own_sem,
     *chunks,
 ):
     sta = lax.axis_index("sta")
@@ -72,19 +70,28 @@
         starts = (0,)
     tabs, gives, gots = chunks[0::3], chunks[1::3], chunks[2::3]
 
-    def table_copy(c, mine):
+    def fill(c, mine):
         rows = pl.ds(pl.multiple_of(starts[c], 16), sizes[c])
-        return pltpu.make_async_copy(
-            table_ref.at[freq if mine else other, :, :, rows, :], tabs[c].at[mine],
-            tab_sem.at[c, mine],
-        )
+        band = freq if mine else other
+        base_cos = table_ref[band, 0, 0, rows, :]
+        base_sin = table_ref[band, 0, 1, rows, :]
+        turn_cos = table_ref[band, 1, 0, rows, :]
+        turn_sin = table_ref[band, 1, 1, rows, :]
+        for q in range(PAD // 128):
+            at_cos = turn_cos[:, q:q + 1]
+            at_sin = turn_sin[:, q:q + 1]
+            lane = slice(q * 128, (q + 1) * 128)
+            waves = (
+                base_cos * at_cos + base_sin * at_sin,
+                base_sin * at_cos - base_cos * at_sin,
+            )
+            for part in range(2):
+                high, low = split(waves[part])
+                tabs[c][mine, 0, part, :, lane] = high
+                tabs[c][mine, 1, part, :, lane] = low
 
     raw_copy = pltpu.make_async_copy(x_ref, raw, raw_sem)
     raw_copy.start()
-    for c in range(len(sizes)):
-        for mine in range(2):
-            table_copy(c, mine).start()
-
     barrier = pltpu.get_barrier_semaphore()
     pl.semaphore_signal(barrier, inc=1, device_id={"freq": other}, device_id_type=MESH)
     for hop in range(1, wins):
@@ -118,12 +125,14 @@
     xh[samples:] = blank
     xl[samples:] = blank
 
+    for mine in range(2):
+        fill(0, mine)
+
     ends = jnp.where(has_right, 1, 0) + jnp.where(has_left, 1, 0)
     pl.semaphore_wait(barrier, wins + ends)
 
     def partial(c, mine):
         rows = sizes[c]
-        table_copy(c, mine).wait()
         odd = lax.broadcasted_iota(jnp.int32, (2 * rows, 1), 0) % 2
         sign = jnp.where((odd == 0) & (freq == 1), -1.0, 1.0).astype(jnp.float32)
         both = dot(tabs[c][mine].reshape(4 * rows, PAD), xh[...])
@@ -238,6 +247,9 @@
     transform(0)
     encode(0, starts[0], sizes[0])
     depart(0)
+    for c in range(1, len(sizes)):
+        for mine in range(2):
+            fill(c, mine)
     keep = pltpu.make_async_copy(codes.at[0], out_ref.at[sta, win], own_sem)
     keep.start()
     early = min(2, stas)
@@ -291,7 +303,9 @@
     return pl.pallas_call(
         functools.partial(spectra_kernel, stas, wins, local_wins),
         out_shape=jax.ShapeDtypeStruct((stas, wins, rows, lanes), jnp.int32),
-        in_specs=[pl.BlockSpec(memory_space=pltpu.SMEM), hold, hold],
+        in_specs=[
+            pl.BlockSpec(memory_space=pltpu.SMEM), hold, pl.BlockSpec(memory_space=pltpu.VMEM),
+        ],
         out_specs=pl.BlockSpec(memory_space=pltpu.VMEM),
         scratch_shapes=[
             pltpu.VMEM((local_wins, samples, lanes), jnp.float32),
@@ -300,7 +314,7 @@
             pltpu.VMEM((2, ROWS, cols), jnp.float32),
             pltpu.VMEM((ROWS, cols), jnp.float32),
             pltpu.VMEM((wins, rows, lanes), jnp.int32),
-            dma(()), dma((2, 2)), dma((2,)), dma((2,)), dma((wins,)), dma((wins,)),
+            dma(()), dma((2,)), dma((2,)), dma((wins,)), dma((wins,)),
             dma((stas, wins)), dma((stas, wins)), dma((stas, wins)), dma((stas, wins)), dma(()),
         ] + chunks,
         compiler_params=pltpu.CompilerParams(
@@ -411,5 +425,5 @@
 def solution(mesh):
     in_specs = (P(("group", "sta"), "win", "freq"), P(("group", "sta")), P("group", None))
     out_specs = P(("group", "sta"), "freq", "win", None, None, None)
-    body = functools.partial(local, dft_table())
+    body = functools.partial(local, dft_factors())
     return jax.shard_map(body, mesh=mesh, in_specs=in_specs, out_specs=out_specs, check_vma=False)

time: 43.6 us -> 44.7 us (1.025)
  Pallas kernels: 42 us -> 43.1 us
    pallas_call x1, Pallas kernels: 35.2 us -> 36.2 us  [gathered_codes(): pl.pallas_call(functools.partial(spectra_kernel, stas, wins, local_wins),...]
where the time goes in v4:
time: 44.7 us; the launch traced here: 44.5 us
  Pallas kernels  43.1 us (96%)
  local copies, waits for them, and re-layouts  0.75 us (2%)
  between operations  0.68 us (2%)
    pallas_call x1, Pallas kernels, gathered_codes(): pl.pallas_call(functools.partial(spectra_kernel, stas, wins, local_wins),...  36.2 us
    pallas_call x1, Pallas kernels, pair_products(): pl.pallas_call(functools.partial(pair_kernel, wins, local_wins, group, bi...  6.85 us

profile of v4, /device:TPU:0, one launch (start us, length us, event | category | flops | bytes accessed | tf_op | source)
XLA Modules:
  0.0 44.5 jit_solution(605653901542873907)
XLA Ops:
  0.0 0.0 copy-start
  0.7 0.0 copy-done
  0.7 0.1 constant_dynamic-slice_fusion
  0.8 0.7 %copy.6.slots_ref = s32[1,2]{1,0:T(1,128)} copy(s32[1,2]{0,1:T(2,128)S(1)} %constant_dynamic-slice_fusion) | data formatting | bytes 16
  1.4 36.2 %spectra.1.left_ref.right_ref = s32[4,2,264,128]{3,2,1,0:T(8,128)} custom-call(s32[1]{0:T(128)S(6)} %copy.7.live_ref, f32[2,1800,128]{2,1,0:T(8,128)} %bitcast.2, f32[2,2,2,272,128]{4,3,2,1,0:T(8,128)} %constant.11.clone.table_ref), custom_call_target="tpu_custom_call" | custom-call | tf_op jit(solution)/shard_map/spectra/pallas_call | solution.py:303
  37.7 6.9 %pairs.1 = bf16[1,128,2,128,128]{4,3,2,1,0:T(8,128)(2,1)} custom-call(s32[1,2]{1,0:T(1,128)} %copy.6.slots_ref, s32[4,2,264,128]{3,2,1,0:T(8,128)} %spectra.1.left_ref.right_ref, s32[4,2,264,128]{3,2,1,0:T(8,128)} %spectra.1.left_ref.right_ref), custom_call_target="tpu_custom_call" | custom-call | tf_op jit(solution)/shard_map/pairs/pallas_call | solution.py:408
Async XLA Ops:
  0.0 0.7 %copy-start = (s32[4,2]{0,1:T(2,128)S(1)}, s32[4,2]{0,1:T(2,128)}, u32[]{:S(2)}) copy-start(s32[4,2]{0,1:T(2,128)} %param.6) | copy-start | bytes 100

commit v5 on v2

--- a/solution.py
+++ b/solution.py
@@ -276,7 +276,7 @@
             dma((stas, wins)), dma((stas, wins)), dma((stas, wins)), dma((stas, wins)), dma(()),
         ],
         compiler_params=pltpu.CompilerParams(
-            collective_id=0, has_side_effects=True, vmem_limit_bytes=61 << 20
+            collective_id=0, has_side_effects=True, vmem_limit_bytes=48 << 20
         ),
         name="spectra",
     )(live, x, table)

time: 42.2 us -> 41 us (0.972)
  Pallas kernels: 39.9 us -> 38.5 us
    pallas_call x1, Pallas kernels: 34.2 us -> 32.8 us  [gathered_codes(): pl.pallas_call(functools.partial(spectra_kernel, stas, wins, local_wins),...]
where the time goes in v5:
time: 41 us; the launch traced here: 40.8 us
  Pallas kernels  38.5 us (94%)
  local copies, waits for them, and re-layouts  1.68 us (4%)
  between operations  0.68 us (2%)
    pallas_call x1, Pallas kernels, gathered_codes(): pl.pallas_call(functools.partial(spectra_kernel, stas, wins, local_wins),...  32.8 us
    pallas_call x1, Pallas kernels, pair_products(): pl.pallas_call(functools.partial(pair_kernel, wins, local_wins, group, bi...  5.68 us
    unnamed x5, local copies, waits for them, and re-layouts  1.61 us

profile of v5, /device:TPU:0, one launch (start us, length us, event | category | flops | bytes accessed | tf_op | source)
XLA Modules:
  0.0 40.8 jit_solution(13268581999404650194)
XLA Ops:
  0.0 0.0 copy-start
  0.7 0.0 copy-done
  0.7 0.1 constant_dynamic-slice_fusion
  0.8 0.1 copy.6.slots_ref
  0.8 0.0 copy-start.1
  0.9 1.5 %copy-done.1 = f32[128,2,1800]{0,2,1:T(8,128)S(1)} copy-done((f32[128,2,1800]{0,2,1:T(8,128)S(1)}, f32[128,2,1800]{0,2,1:T(8,128)}, u32[]{:S(2)}) %copy-start.1) | copy-done | bytes 1843224
  2.4 32.8 %spectra.1.left_ref.right_ref = s32[4,2,264,128]{3,2,1,0:T(8,128)S(1)} custom-call(s32[1]{0:T(128)S(6)} %copy.7.live_ref, f32[2,1800,128]{2,1,0:T(8,128)S(1)} %bitcast.2, bf16[2,2,2,272,1920]{4,3,2,1,0:T(8,128)(2,1)} %constant.11.clone.table_ref), custom_call_target="tpu_custom_call" | custom-call | tf_op jit(solution)/shard_map/spectra/pallas_call | solution.py:261
  35.1 5.7 %pairs.1 = bf16[1,128,2,128,128]{4,3,2,1,0:T(8,128)(2,1)} custom-call(s32[1,2]{1,0:T(1,128)S(1)} %copy.6.slots_ref, s32[4,2,264,128]{3,2,1,0:T(8,128)S(1)} %spectra.1.left_ref.right_ref, s32[4,2,264,128]{3,2,1,0:T(8,128)S(1)} %spectra.1.left_ref.right_ref), custom_call_target="tpu_custom_call" | custom-call | tf_op jit(solution)/shard_map/pairs/pallas_call | solution.py:366
Async XLA Ops:
  0.0 0.7 %copy-start = (s32[4,2]{0,1:T(2,128)S(1)}, s32[4,2]{0,1:T(2,128)}, u32[]{:S(2)}) copy-start(s32[4,2]{0,1:T(2,128)} %param.6) | copy-start | bytes 100
  0.8 1.5 %copy-start.1 = (f32[128,2,1800]{0,2,1:T(8,128)S(1)}, f32[128,2,1800]{0,2,1:T(8,128)}, u32[]{:S(2)}) copy-start(f32[128,2,1800]{0,2,1:T(8,128)} %param.4) | copy-start | bytes 5529604
